TPU v7x, 128 devices: a whole 4x4x4 slice. The times are simulated.
128 devices in a mesh: blk: 16 (over y, x_hi, core), rep: 8 (over x_lo, z).
Axes of the slice: x: 4 (x_hi: 2, x_lo: 2; x = x_hi * 2 + x_lo), y: 4, z: 4, core: 2. Of those that a mesh axis runs over, the one named last changes fastest.
Arguments:
- cotangent: bfloat16 [512, 256, 128], P('blk', 'rep'), may hold values from -6 to 6
- relu_mask: int32 [512, 256, 128], P('blk', 'rep'), may hold values 0 or 1
- aggregated: bfloat16 [512, 256, 128], P('blk', 'rep'), may hold values from -6 to 6
- weight: bfloat16 [256, 256], P('rep'), may hold values from -0.375 to 0.375
- tiles: bfloat16 [512, 16, 128, 128], P('blk'), may hold values from -0.125 to 0.125
- col_block: int32 [512, 16], P('blk'), may hold values from 0 to 511, as said below
- live_count: int32 [512], P('blk'), may hold values from 1 to 16, as said below
Outputs:
- input_grad: bfloat16 [512, 256, 128], P('blk', 'rep')
- weight_grad: float32 [256, 256], P('rep')
Inputs may be any that keep to these rules, and one draw needn't show every extreme that they name: The slab of a row block b is b // 32; the slab of col_block[b, s] lies at most 2 slabs from it around the closed cycle of the 16 slabs, and both distance 2 directions occur. `live_count`: row blocks of one slab share a density level, so live counts differ from slab to slab; some row block has all 16 slots live.
All inputs are finite; a program needn't handle non-finite values. No bound on the sum of `relu_mask` on one device may be relied on, other than what follows from the above.
Results may differ from a plain program's by a relative error of at most 0.0049.
Values may be sent and summed in bfloat16 or wider, within the bound.
A program may use at most 128 MiB of HBM per device.

v0:
```python
import math
import jax
import jax.numpy as jnp
from jax import lax
from jax.sharding import PartitionSpec as P

REACH = 2


def from_behind(value, axis, steps):
    count = lax.axis_size(axis)
    pairs = [(source, (source + steps) % count) for source in range(count)]
    return lax.ppermute(value, axis, pairs)


def on_device(cotangent, relu_mask, aggregated, weight, tiles, col_block, live_count):
    blocks_here = cotangent.shape[0]
    cols_here = cotangent.shape[1]
    tile_size = cotangent.shape[2]
    grad_z = cotangent * relu_mask.astype(jnp.bfloat16)
    gathered_part = lax.all_gather(grad_z, "rep", axis=1, tiled=True)
    grad_h = jnp.einsum("io,bon->bin", weight, gathered_part, preferred_element_type=jnp.float32)
    col_part = jnp.einsum(
        "bin,bon->io", aggregated, gathered_part, preferred_element_type=jnp.float32
    )
    grad_w = col_part
    grad_h, grad_w = (grad_h, grad_w)
    nodes_all = lax.axis_size("blk") * blocks_here * tile_size
    weight_grad = lax.psum(grad_w, "blk") * (1.0 / math.sqrt(nodes_all))
    grad_hb = grad_h.astype(jnp.bfloat16)
    slot_count = tiles.shape[1]
    slot_ids = jnp.arange(slot_count, dtype=jnp.int32)
    live = (slot_ids[None, :] < live_count[:, None]).astype(jnp.float32).reshape(-1)
    contrib = jnp.einsum("bkij,bfi->bkfj", tiles, grad_hb, preferred_element_type=jnp.float32)
    flat_terms = contrib.reshape(blocks_here * slot_count, cols_here * tile_size)
    targets = col_block.reshape(-1)
    slabs = lax.axis_size("blk")
    own_slab = lax.axis_index("blk")
    target_slab = targets // blocks_here
    window_slot = (target_slab - own_slab + REACH + slabs) % slabs
    position = window_slot * blocks_here + targets % blocks_here
    window_rows = (2 * REACH + 1) * blocks_here
    row_ids = jnp.arange(window_rows, dtype=jnp.int32)
    selector = (position[None, :] == row_ids[:, None]).astype(jnp.float32) * live[None, :]
    window = jnp.dot(
        selector, flat_terms, preferred_element_type=jnp.float32, precision=lax.Precision.HIGHEST
    )
    window = window.reshape(2 * REACH + 1, blocks_here, cols_here, tile_size)
    input_grad = window[REACH]
    upward = window[2 * REACH]
    downward = window[0]
    for step in range(REACH):
        upward = from_behind(upward, "blk", 1)
        downward = from_behind(downward, "blk", -1)
        if step + 1 < REACH:
            upward = upward + window[2 * REACH - step - 1]
            downward = downward + window[step + 1]
    input_grad = input_grad + upward + downward
    return (input_grad.astype(jnp.bfloat16), weight_grad)


def solution(mesh):
    placed = (
        P("blk", "rep", None),
        P("blk", "rep", None),
        P("blk", "rep", None),
        P("rep", None),
        P("blk", None, None, None),
        P("blk", None),
        P("blk"),
    )
    return jax.shard_map(
        on_device,
        mesh=mesh,
        in_specs=placed,
        out_specs=(P("blk", "rep", None), P("rep", None)),
        check_vma=False,
    )
```

profile of v0, /device:TPU:0, one launch (start us, length us, event | category | flops | bytes accessed | tf_op | source)
XLA Modules:
  0.0 174.0 jit_solution(14960853211397327882)
XLA Ops:
  7.2 0.0 copy-start
  7.2 0.0 all-gather.2.cloned.1.call-start
  7.2 1.9 %convert_multiply_fusion = bf16[32,32,128]{2,1,0:T(8,128)(2,1)} fusion(bf16[32,32,128]{2,1,0:T(8,128)(2,1)} %param.7, s32[32,32,128]{2,1,0:T(8,128)} %param.8), kind=kLoop, calls=%fused_computation.19 | loop fusion | flops 262144 | bytes 1048576 | tf_op jit(solution)/shard_map/mul | solution.py:20
  9.1 0.0 all-gather.2.cloned.1.call-update
  9.1 0.8 copy.9
  9.9 0.1 reshape.102
  10.0 0.7 fusion.13
  10.7 0.1 reshape.104
  10.8 43.8 %all-gather.2.cloned.1.call-done = bf16[32,256,128]{2,1,0:T(8,128)(2,1)} async-done(((bf16[32,32,128]{2,1,0:T(8,128)(2,1)}), bf16[32,256,128]{2,1,0:T(8,128)(2,1)}) %all-gather.2.cloned.1.call-update) | async-done | bytes 2097168 | tf_op jit(solution)/shard_map/all_gather | solution.py:21
  54.6 9.9 %fusion.4 = f32[32,32,16,128]{3,1,2,0:T(8,128)} fusion(bf16[32,16,128,128]{3,2,1,0:T(8,128)(2,1)} %param.11, bf16[32,256,128]{2,1,0:T(8,128)(2,1)} %all-gather.2.cloned.1.call-done, bf16[32,256]{1,0:T(8,128)(2,1)} %param.10), kind=kOutput, calls=%fused_computation.6 | convolution fusion | flops 604110848 | bytes 27279360 | tf_op jit(solution)/shard_map/bkij,bfi->bkfj/dot_general | solution.py:34
  64.5 11.3 %fusion = f32[160,4096]{1,0:T(8,128)S(1)} fusion(f32[64,8,32,128]{3,2,1,0:T(8,128)} %bitcast.46, f32[512]{0:T(512)S(1)} %reshape.104, s32[512]{0:T(512)S(1)} %fusion.18), kind=kOutput, calls=%fused_computation | convolution fusion | flops 4026695680 | bytes 11014144 | tf_op jit(solution)/shard_map/dot_general | solution.py:45
  75.9 0.2 slice_bitcast_fusion.4
  76.0 0.1 copy.13
  76.1 0.1 collective-permute-start
  76.2 0.1 copy.15
  76.3 5.4 %collective-permute-start.2 = (f32[32,32,128]{2,1,0:T(8,128)S(1)}, f32[32,32,128]{2,1,0:T(8,128)S(1)}, u32[]{:S(2)}, u32[]{:S(2)}) collective-permute-start(f32[32,32,128]{2,1,0:T(8,128)S(1)} %bitcast.47), channel_id=1, source_target_pairs={{0,120},{8,0},{16,8},{24,16},{32,24},{40,32},{48,40},{56,48},{64,5... | collective-permute-start | bytes 1572872 | tf_op jit(solution)/shard_map/ppermute | solution.py:13
  81.7 0.1 copy.16
  81.8 0.0 copy-start.1
  81.8 0.1 copy.14
  81.9 8.8 %collective-permute-done = f32[32,32,128]{2,1,0:T(8,128)S(1)} collective-permute-done((f32[32,32,128]{2,1,0:T(8,128)S(1)}, f32[32,32,128]{2,1,0:T(8,128)S(1)}, u32[]{:S(2)}, u32[]{:S(2)}) %collective-permute-start) | collective-permute-done | bytes 524320 | tf_op jit(solution)/shard_map/ppermute | solution.py:13
  90.8 0.1 bitcast_add_fusion.1
  90.9 0.1 collective-permute-start.1
  90.9 0.0 collective-permute-done.2
  91.0 0.1 bitcast_add_fusion
  91.0 5.4 %collective-permute-start.3 = (f32[32,32,128]{2,1,0:T(8,128)S(1)}, f32[32,32,128]{2,1,0:T(8,128)S(1)}, u32[]{:S(2)}, u32[]{:S(2)}) collective-permute-start(f32[32,32,128]{2,1,0:T(8,128)S(1)} %bitcast_add_fusion), channel_id=1, source_target_pairs={{0,120},{8,0},{16,8},{24,16},{32,24},{40,32},{48,40},{56,48},{64,5... | collective-permute-start | bytes 1572872 | tf_op jit(solution)/shard_map/ppermute | solution.py:13
  96.4 0.1 copy.12
  96.5 0.0 copy-done
  96.6 0.0 copy-done.1
  96.6 0.7 convolution_bitcast_fusion
  97.3 68.4 %psum.7 = f32[32,256]{1,0:T(8,128)S(1)} all-reduce(f32[32,256]{1,0:T(8,128)S(1)} %convolution_bitcast_fusion), channel_id=1, replica_groups=mesh['blk'=16,'rep'=8] {'blk'}, use_global_device_ids=true, to_apply=%region_0.0 | all-reduce | flops 8192 | bytes 65536 | tf_op jit(solution)/shard_map/psum | solution.py:29
  165.6 0.6 broadcast_multiply_fusion
  166.2 0.0 collective-permute-done.1
  166.2 0.0 collective-permute-done.3
  166.3 0.9 fusion.6
  (1 shorter events, 0.0 us)
Async XLA Ops:
  7.2 89.4 %copy-start = (bf16[32,32,128]{2,1,0:T(8,128)(2,1)S(1)}, bf16[32,32,128]{2,1,0:T(8,128)(2,1)}, u32[]{:S(2)}) copy-start(bf16[32,32,128]{2,1,0:T(8,128)(2,1)} %param.9) | copy-start | bytes 786436
  7.2 47.5 %all-gather.2.cloned.1.call-start = ((), (), s32[]{:S(2)}) async-start(), calls=%async_computation | async-start | bytes 2359296 | tf_op jit(solution)/shard_map/all_gather | solution.py:21
  76.1 14.6 %collective-permute-start = (f32[32,32,128]{2,1,0:T(8,128)S(1)}, f32[32,32,128]{2,1,0:T(8,128)S(1)}, u32[]{:S(2)}, u32[]{:S(2)}) collective-permute-start(f32[32,32,128]{2,1,0:T(8,128)S(1)} %bitcast.48), channel_id=1, source_target_pairs={{0,8},{8,16},{16,24},{24,32},{32,40},{40,48},{48,56},{56,64},{64,7... | collective-permute-start | bytes 1572872 | tf_op jit(solution)/shard_map/ppermute | solution.py:13
  76.3 14.6 %collective-permute-start.2 = (f32[32,32,128]{2,1,0:T(8,128)S(1)}, f32[32,32,128]{2,1,0:T(8,128)S(1)}, u32[]{:S(2)}, u32[]{:S(2)}) collective-permute-start(f32[32,32,128]{2,1,0:T(8,128)S(1)} %bitcast.47), channel_id=1, source_target_pairs={{0,120},{8,0},{16,8},{24,16},{32,24},{40,32},{48,40},{56,48},{64,5... | collective-permute-start | bytes 1572872 | tf_op jit(solution)/shard_map/ppermute | solution.py:13
  81.8 14.7 %copy-start.1 = (bf16[32,256,128]{2,1,0:T(8,128)(2,1)S(1)}, bf16[32,256,128]{2,1,0:T(8,128)(2,1)}, u32[]{:S(2)}) copy-start(bf16[32,256,128]{2,1,0:T(8,128)(2,1)} %all-gather.2.cloned.1.call-done) | copy-start | bytes 6291460
  90.9 75.4 %collective-permute-start.1 = (f32[32,32,128]{2,1,0:T(8,128)S(1)}, f32[32,32,128]{2,1,0:T(8,128)S(1)}, u32[]{:S(2)}, u32[]{:S(2)}) collective-permute-start(f32[32,32,128]{2,1,0:T(8,128)S(1)} %bitcast_add_fusion.1), channel_id=1, source_target_pairs={{0,8},{8,16},{16,24},{24,32},{32,40},{40,48},{48,56},{56,64},{64,7... | collective-permute-start | bytes 1572872 | tf_op jit(solution)/shard_map/ppermute | solution.py:13
  91.0 75.2 %collective-permute-start.3 = (f32[32,32,128]{2,1,0:T(8,128)S(1)}, f32[32,32,128]{2,1,0:T(8,128)S(1)}, u32[]{:S(2)}, u32[]{:S(2)}) collective-permute-start(f32[32,32,128]{2,1,0:T(8,128)S(1)} %bitcast_add_fusion), channel_id=1, source_target_pairs={{0,120},{8,0},{16,8},{24,16},{32,24},{40,32},{48,40},{56,48},{64,5... | collective-permute-start | bytes 1572872 | tf_op jit(solution)/shard_map/ppermute | solution.py:13
Sparse Core Ops, SparseCore 0:
  10.2 44.3 all-gather.1
where the time goes:
time: 174 us
  blocking collectives  68.4 us (39%)
  waiting for transfers between devices  52.7 us (30%)
  matrix products  21.9 us (13%)
  between operations  14.1 us (8%)
  starting transfers between devices  11 us (6%)
  other arithmetic  4.3 us (2%)
    psum x1, blocking collectives, on_device(): weight_grad = lax.psum(grad_w, 'blk') * (1.0 / math.sqrt(nodes_all))  68.4 us
    all_gather x1, waiting for transfers between devices, on_device(): gathered_part = lax.all_gather(grad_z, 'rep', axis=1, tiled=True)  43.8 us
    dot_general x1, matrix products, on_device(): jnp.dot(selector, flat_terms, preferred_element_type=jnp.float32, precisi...  11.3 us
    ppermute x4, starting transfers between devices, from_behind(): return lax.ppermute(value, axis, pairs)  11 us
    dot_general x1, matrix products, on_device(): jnp.einsum('bkij,bfi->bkfj', tiles, grad_hb, preferred_element_type=jnp.f...  9.9 us
    ppermute x4, waiting for transfers between devices, from_behind(): return lax.ppermute(value, axis, pairs)  8.83 us
  transfers between devices with their start and end apart: 5, of which 2 were waited for; matrix products, arithmetic and copies ran while one was open for 2% of the time, Pallas kernels for 0%

commit v1 on v0

--- a/solution.py
+++ b/solution.py
@@ -26,7 +26,7 @@
     grad_w = col_part
     grad_h, grad_w = (grad_h, grad_w)
     nodes_all = lax.axis_size("blk") * blocks_here * tile_size
-    weight_grad = lax.psum(grad_w, "blk") * (1.0 / math.sqrt(nodes_all))
+    weight_grad = jnp.sum(lax.all_gather(grad_w, "blk"), axis=0) * (1.0 / math.sqrt(nodes_all))
     grad_hb = grad_h.astype(jnp.bfloat16)
     slot_count = tiles.shape[1]
     slot_ids = jnp.arange(slot_count, dtype=jnp.int32)

time: 174 us -> 134 us (0.77)
  blocking collectives: 68.4 us -> 26.7 us
    psum x1 -> x0, blocking collectives: 68.4 us -> none  [on_device(): weight_grad = lax.psum(grad_w, 'blk') * (1.0 / math.sqrt(nodes_all))]
    all_gather x0 -> x1, blocking collectives: none -> 26.7 us  [on_device(): lax.all_gather(grad_w, 'blk')]
  transfers between devices with their start and end apart: 5 -> 5, of which waited for: 2 -> 2; matrix products, arithmetic and copies ran while one was open for 2% -> 3% of each run, Pallas kernels for 0% -> 0%
where the time goes in v1:
time: 134 us; the launch traced here: 132 us
  waiting for transfers between devices  52.7 us (39%)
  blocking collectives  26.7 us (20%)
  matrix products  21.9 us (16%)
  between operations  14.1 us (11%)
  starting transfers between devices  11 us (8%)
  other arithmetic  4.33 us (3%)
  local copies, waits for them, and re-layouts  1.62 us (1%)
    all_gather x1, waiting for transfers between devices, on_device(): gathered_part = lax.all_gather(grad_z, 'rep', axis=1, tiled=True)  43.8 us
    all_gather x1, blocking collectives, on_device(): lax.all_gather(grad_w, 'blk')  26.7 us
    dot_general x1, matrix products, on_device(): jnp.dot(selector, flat_terms, preferred_element_type=jnp.float32, precisi...  11.3 us
    ppermute x4, starting transfers between devices, from_behind(): return lax.ppermute(value, axis, pairs)  11 us
    dot_general x1, matrix products, on_device(): jnp.einsum('bkij,bfi->bkfj', tiles, grad_hb, preferred_element_type=jnp.f...  9.9 us
    ppermute x4, waiting for transfers between devices, from_behind(): return lax.ppermute(value, axis, pairs)  8.84 us
  transfers between devices with their start and end apart: 5, of which 2 were waited for; matrix products, arithmetic and copies ran while one was open for 3% of the time, Pallas kernels for 0%

profile of v1, /device:TPU:0, one launch (start us, length us, event | category | flops | bytes accessed | tf_op | source)
XLA Modules:
  0.0 132.4 jit_solution(11192166214948981971)
XLA Ops:
  7.2 0.0 copy-start
  7.2 0.0 all-gather.3.cloned.1.call-start
  7.2 1.9 %convert_multiply_fusion = bf16[32,32,128]{2,1,0:T(8,128)(2,1)} fusion(bf16[32,32,128]{2,1,0:T(8,128)(2,1)} %param.7, s32[32,32,128]{2,1,0:T(8,128)} %param.8), kind=kLoop, calls=%fused_computation.19 | loop fusion | flops 262144 | bytes 1048576 | tf_op jit(solution)/shard_map/mul | solution.py:20
  9.1 0.0 all-gather.3.cloned.1.call-update
  9.1 0.8 copy.9
  9.9 0.1 reshape.102
  10.0 0.7 fusion.13
  10.7 0.1 reshape.104
  10.8 43.8 %all-gather.3.cloned.1.call-done = bf16[32,256,128]{2,1,0:T(8,128)(2,1)} async-done(((bf16[32,32,128]{2,1,0:T(8,128)(2,1)}), bf16[32,256,128]{2,1,0:T(8,128)(2,1)}) %all-gather.3.cloned.1.call-update) | async-done | bytes 2097168 | tf_op jit(solution)/shard_map/all_gather | solution.py:21
  54.6 9.9 %fusion.4 = f32[32,32,16,128]{3,1,2,0:T(8,128)} fusion(bf16[32,16,128,128]{3,2,1,0:T(8,128)(2,1)} %param.11, bf16[32,256,128]{2,1,0:T(8,128)(2,1)} %all-gather.3.cloned.1.call-done, bf16[32,256]{1,0:T(8,128)(2,1)} %param.10), kind=kOutput, calls=%fused_computation.6 | convolution fusion | flops 604110848 | bytes 27279360 | tf_op jit(solution)/shard_map/bkij,bfi->bkfj/dot_general | solution.py:34
  64.5 11.3 %fusion = f32[160,4096]{1,0:T(8,128)S(1)} fusion(f32[64,8,32,128]{3,2,1,0:T(8,128)} %bitcast.47, f32[512]{0:T(512)S(1)} %reshape.104, s32[512]{0:T(512)S(1)} %fusion.18), kind=kOutput, calls=%fused_computation | convolution fusion | flops 4026695680 | bytes 11014144 | tf_op jit(solution)/shard_map/dot_general | solution.py:45
  75.9 0.2 slice_bitcast_fusion.4
  76.0 0.1 copy.13
  76.1 0.1 collective-permute-start
  76.2 0.1 copy.15
  76.3 5.4 %collective-permute-start.2 = (f32[32,32,128]{2,1,0:T(8,128)S(1)}, f32[32,32,128]{2,1,0:T(8,128)S(1)}, u32[]{:S(2)}, u32[]{:S(2)}) collective-permute-start(f32[32,32,128]{2,1,0:T(8,128)S(1)} %bitcast.49), channel_id=1, source_target_pairs={{0,120},{8,0},{16,8},{24,16},{32,24},{40,32},{48,40},{56,48},{64,5... | collective-permute-start | bytes 1572872 | tf_op jit(solution)/shard_map/ppermute | solution.py:13
  81.7 0.0 copy-start.1
  81.7 0.1 copy.16
  81.8 0.1 copy.14
  81.9 8.8 %collective-permute-done = f32[32,32,128]{2,1,0:T(8,128)S(1)} collective-permute-done((f32[32,32,128]{2,1,0:T(8,128)S(1)}, f32[32,32,128]{2,1,0:T(8,128)S(1)}, u32[]{:S(2)}, u32[]{:S(2)}) %collective-permute-start) | collective-permute-done | bytes 524320 | tf_op jit(solution)/shard_map/ppermute | solution.py:13
  90.8 0.1 bitcast_add_fusion.1
  90.9 0.1 collective-permute-start.1
  90.9 0.0 collective-permute-done.2
  91.0 0.1 bitcast_add_fusion
  91.0 5.4 %collective-permute-start.3 = (f32[32,32,128]{2,1,0:T(8,128)S(1)}, f32[32,32,128]{2,1,0:T(8,128)S(1)}, u32[]{:S(2)}, u32[]{:S(2)}) collective-permute-start(f32[32,32,128]{2,1,0:T(8,128)S(1)} %bitcast_add_fusion), channel_id=1, source_target_pairs={{0,120},{8,0},{16,8},{24,16},{32,24},{40,32},{48,40},{56,48},{64,5... | collective-permute-start | bytes 1572872 | tf_op jit(solution)/shard_map/ppermute | solution.py:13
  96.4 0.0 copy-done
  96.5 0.0 copy-done.1
  96.5 0.7 convolution_bitcast_fusion
  97.2 0.1 copy.12
  97.3 26.7 %all-gather = f32[512,256]{1,0:T(8,128)S(1)} all-gather(f32[32,256]{1,0:T(8,128)S(1)} %convolution_bitcast_fusion), channel_id=2, replica_groups=mesh['blk'=16,'rep'=8] {'blk'}, dimensions={0}, use_global_device_ids=true | all-gather | bytes 557056 | tf_op jit(solution)/shard_map/all_gather | solution.py:29
  124.0 0.6 broadcast_multiply_fusion
  124.7 0.0 collective-permute-done.1
  124.7 0.0 collective-permute-done.3
  124.7 0.9 fusion.6
  (2 shorter events, 0.1 us)
Async XLA Ops:
  7.2 89.3 %copy-start = (bf16[32,32,128]{2,1,0:T(8,128)(2,1)S(1)}, bf16[32,32,128]{2,1,0:T(8,128)(2,1)}, u32[]{:S(2)}) copy-start(bf16[32,32,128]{2,1,0:T(8,128)(2,1)} %param.9) | copy-start | bytes 786436
  7.2 47.5 %all-gather.3.cloned.1.call-start = ((), (), s32[]{:S(2)}) async-start(), calls=%async_computation | async-start | bytes 2359296 | tf_op jit(solution)/shard_map/all_gather | solution.py:21
  76.1 14.6 %collective-permute-start = (f32[32,32,128]{2,1,0:T(8,128)S(1)}, f32[32,32,128]{2,1,0:T(8,128)S(1)}, u32[]{:S(2)}, u32[]{:S(2)}) collective-permute-start(f32[32,32,128]{2,1,0:T(8,128)S(1)} %bitcast.50), channel_id=1, source_target_pairs={{0,8},{8,16},{16,24},{24,32},{32,40},{40,48},{48,56},{56,64},{64,7... | collective-permute-start | bytes 1572872 | tf_op jit(solution)/shard_map/ppermute | solution.py:13
  76.3 14.6 %collective-permute-start.2 = (f32[32,32,128]{2,1,0:T(8,128)S(1)}, f32[32,32,128]{2,1,0:T(8,128)S(1)}, u32[]{:S(2)}, u32[]{:S(2)}) collective-permute-start(f32[32,32,128]{2,1,0:T(8,128)S(1)} %bitcast.49), channel_id=1, source_target_pairs={{0,120},{8,0},{16,8},{24,16},{32,24},{40,32},{48,40},{56,48},{64,5... | collective-permute-start | bytes 1572872 | tf_op jit(solution)/shard_map/ppermute | solution.py:13
  81.7 14.7 %copy-start.1 = (bf16[32,256,128]{2,1,0:T(8,128)(2,1)S(1)}, bf16[32,256,128]{2,1,0:T(8,128)(2,1)}, u32[]{:S(2)}) copy-start(bf16[32,256,128]{2,1,0:T(8,128)(2,1)} %all-gather.3.cloned.1.call-done) | copy-start | bytes 6291460
  90.9 33.8 %collective-permute-start.1 = (f32[32,32,128]{2,1,0:T(8,128)S(1)}, f32[32,32,128]{2,1,0:T(8,128)S(1)}, u32[]{:S(2)}, u32[]{:S(2)}) collective-permute-start(f32[32,32,128]{2,1,0:T(8,128)S(1)} %bitcast_add_fusion.1), channel_id=1, source_target_pairs={{0,8},{8,16},{16,24},{24,32},{32,40},{40,48},{48,56},{56,64},{64,7... | collective-permute-start | bytes 1572872 | tf_op jit(solution)/shard_map/ppermute | solution.py:13
  91.0 33.6 %collective-permute-start.3 = (f32[32,32,128]{2,1,0:T(8,128)S(1)}, f32[32,32,128]{2,1,0:T(8,128)S(1)}, u32[]{:S(2)}, u32[]{:S(2)}) collective-permute-start(f32[32,32,128]{2,1,0:T(8,128)S(1)} %bitcast_add_fusion), channel_id=1, source_target_pairs={{0,120},{8,0},{16,8},{24,16},{32,24},{40,32},{48,40},{56,48},{64,5... | collective-permute-start | bytes 1572872 | tf_op jit(solution)/shard_map/ppermute | solution.py:13
Sparse Core Ops, SparseCore 0:
  10.2 44.3 all-gather.2
